TPU v7x, 32 devices: a whole 2x2x4 slice. The times are simulated.
32 devices in a mesh: bx: 8 (over z, x), by: 4 (over y, core).
Axes of the slice: x: 2, y: 2, z: 4, core: 2. Of those that a mesh axis runs over, the one named last changes fastest.
Arguments:
- box_map: float32 [8, 4, 256, 256], P('bx', 'by'), as said below
- box_load: float32 [8, 4, 64, 256], P('bx', 'by'), may hold values from -6 to 6
- box_order: int32 [8, 4, 256], P('bx', 'by'), may hold values from 0 to 255, each once within a row
- incoming: float32 [8, 4, 64, 128], P('bx', 'by'), may hold values from -54 to 54
- edge_map: float32 [8, 4, 256, 128], P('bx', 'by'), may hold values from -0.375 to 0.375
- edge_load: float32 [8, 4, 64, 128], P('bx', 'by'), may hold values from -6 to 6
Outputs:
- top_map: float32 [8, 4, 512, 128], P('bx', 'by')
- top_load: float32 [8, 4, 64, 128], P('bx', 'by')
- box_incoming: float32 [8, 4, 64, 256], P('bx', 'by')
- edge_values: float32 [8, 4, 64, 128], P('bx', 'by')
Inputs may be any that keep to these rules, and one draw needn't show every extreme that they name: Each row of box_order holds every number from 0 to 255 once. Every box_map[i, j] has spectral norm at most 0.7.
All inputs are finite; a program needn't handle non-finite values.
Results may differ from a plain program's by a relative error of at most 0.0001.
Values sent between devices are 32-bit elements; how exact they have to be, the bound alone decides.
No kernel may reach another device: no remote copies, remote signals or barrier semaphores. Data moves between devices by JAX's collectives and lax.ppermute only.
A program may use at most 64 MiB of HBM per device.

v0:
```python
import jax
import jax.numpy as jnp
from jax import lax
from jax.sharding import PartitionSpec as P

ALPHA_ORDER = ((0, 2, 3, 1), (0, 3, 2, 1))
BETA_ORDER = ((1, 2, 3, 0), (1, 3, 2, 0))
MACRO_ORDER = (0, 1, 3, 4, 2, 5)


def swapped(block, axis, apart):
    count = lax.axis_size(axis)
    route = []
    for low in range(count):
        high = low | 1 << apart
        if high != low and high < count:
            route += [(low, high), (high, low)]
    return lax.ppermute(block, axis, route)


def matmul(first, second):
    return jnp.dot(
        first, second, precision=lax.Precision.HIGHEST, preferred_element_type=jnp.float32
    )


def block_index(blocks, breadth):
    return jnp.concatenate(
        [jnp.arange(breadth, dtype=jnp.int32) + number * breadth for number in blocks]
    )


def canonical_blocks(order):
    return tuple((order.index(number) for number in range(4)))


def inverse_of(kernel):
    normal_matrix = matmul(kernel.T, kernel)
    factor = jnp.linalg.cholesky(normal_matrix)
    return jax.scipy.linalg.cho_solve((factor, True), kernel.T)


def interface_terms(alpha_outer, alpha_inner, alpha_free, beta_outer, beta_inner, beta_free):
    inner_size = alpha_inner.shape[0]
    kernel = jnp.eye(inner_size, dtype=jnp.float32) - matmul(beta_inner, alpha_inner)
    inverse = inverse_of(kernel)
    alpha_from_alpha = matmul(alpha_outer, inverse)
    alpha_from_beta = -matmul(matmul(beta_outer, alpha_inner), inverse)
    alpha_source = matmul(alpha_free - matmul(beta_free, alpha_inner), inverse)
    beta_from_alpha = -matmul(alpha_from_alpha, beta_inner)
    beta_from_beta = beta_outer - matmul(alpha_from_beta, beta_inner)
    beta_source = beta_free - matmul(alpha_source, beta_inner)
    return (
        alpha_from_alpha,
        alpha_from_beta,
        alpha_source,
        beta_from_alpha,
        beta_from_beta,
        beta_source,
    )


def full_merge(alpha_map, alpha_load, beta_map, beta_load, outer):
    terms = interface_terms(
        alpha_map[:outer, outer:],
        alpha_map[outer:, outer:],
        alpha_load[:, outer:],
        beta_map[:outer, outer:],
        beta_map[outer:, outer:],
        beta_load[:, outer:],
    )
    (
        alpha_from_alpha,
        alpha_from_beta,
        alpha_source,
        beta_from_alpha,
        beta_from_beta,
        beta_source,
    ) = terms
    alpha_back = alpha_map[outer:, :outer]
    beta_back = beta_map[outer:, :outer]
    upper = jnp.concatenate(
        [
            alpha_map[:outer, :outer] - matmul(beta_from_alpha, alpha_back),
            -matmul(alpha_from_alpha, beta_back),
        ],
        axis=1,
    )
    lower = jnp.concatenate(
        [
            -matmul(beta_from_beta, alpha_back),
            beta_map[:outer, :outer] - matmul(alpha_from_beta, beta_back),
        ],
        axis=1,
    )
    merged = jnp.concatenate([upper, lower], axis=0)
    merged_load = jnp.concatenate(
        [
            alpha_load[:, :outer] - matmul(beta_source, alpha_back),
            beta_load[:, :outer] - matmul(alpha_source, beta_back),
        ],
        axis=1,
    )
    return (merged, merged_load, terms)


def interface_values(terms, alpha_in, beta_in):
    (
        alpha_from_alpha,
        alpha_from_beta,
        alpha_source,
        beta_from_alpha,
        beta_from_beta,
        beta_source,
    ) = terms
    alpha_value = (
        matmul(alpha_in, alpha_from_alpha) + matmul(beta_in, alpha_from_beta) + alpha_source
    )
    beta_value = matmul(alpha_in, beta_from_alpha) + matmul(beta_in, beta_from_beta) + beta_source
    return (alpha_value, beta_value)


def body(box_map, box_load, box_order, incoming, edge_map, edge_load):
    own_map = box_map[0, 0]
    own_load = box_load[0, 0]
    own_order = box_order[0, 0]
    raw_incoming = incoming[0, 0]
    own_edge = edge_map[0, 0]
    own_edge_load = edge_load[0, 0]
    breadth = own_map.shape[0] // 4
    share_size = 2 * breadth
    outer = 4 * breadth
    box_total = lax.axis_size("bx") * lax.axis_size("by")
    power = lax.psum(jnp.sum(raw_incoming * raw_incoming, axis=1), ("bx", "by"))
    factor = 1.0 / jnp.sqrt(power / (box_total * raw_incoming.shape[1]) + 1e-06)
    own_incoming = raw_incoming * factor[:, None]
    x_parity = lax.axis_index("bx") % 2
    y_parity = lax.axis_index("by") % 2
    role_index = 2 * x_parity + y_parity
    is_alpha = x_parity == 0
    is_bottom = y_parity == 0
    forward_table = jnp.stack(
        [
            block_index(ALPHA_ORDER[0], breadth),
            block_index(ALPHA_ORDER[1], breadth),
            block_index(BETA_ORDER[0], breadth),
            block_index(BETA_ORDER[1], breadth),
        ]
    )
    picked = jnp.take(own_order, forward_table[role_index], axis=0)
    role_map = jnp.take(jnp.take(own_map, picked, axis=0), picked, axis=1)
    role_load = jnp.take(own_load, picked, axis=1)
    other_map, other_load, other_incoming = swapped((role_map, role_load, own_incoming), "bx", 0)
    alpha_map = jnp.where(is_alpha, role_map, other_map)
    beta_map = jnp.where(is_alpha, other_map, role_map)
    alpha_load = jnp.where(is_alpha, role_load, other_load)
    beta_load = jnp.where(is_alpha, other_load, role_load)
    alpha_incoming = jnp.where(is_alpha, own_incoming, other_incoming)
    beta_incoming = jnp.where(is_alpha, other_incoming, own_incoming)
    level_map, level_load, level_terms = full_merge(
        alpha_map, alpha_load, beta_map, beta_load, 3 * breadth
    )
    macro_index = block_index(MACRO_ORDER, breadth)
    macro_map = jnp.take(jnp.take(level_map, macro_index, axis=0), macro_index, axis=1)
    macro_load = jnp.take(level_load, macro_index, axis=1)
    macro_incoming = jnp.concatenate([alpha_incoming, beta_incoming], axis=1)
    far_outer, far_inner, far_free, far_incoming = swapped(
        (
            macro_map[:outer, outer:],
            macro_map[outer:, outer:],
            macro_load[:, outer:],
            macro_incoming,
        ),
        "by",
        0,
    )
    near_terms = interface_terms(
        macro_map[:outer, outer:],
        macro_map[outer:, outer:],
        macro_load[:, outer:],
        far_outer,
        far_inner,
        far_free,
    )
    near_value, far_value = interface_values(near_terms, macro_incoming, far_incoming)
    macro_inside = -far_value
    start = x_parity * share_size
    own_back = lax.dynamic_slice_in_dim(macro_map[outer:, :outer], start, share_size, 1)
    own_columns = lax.dynamic_slice_in_dim(macro_map[:outer, :outer], start, share_size, 1)
    near_rows = own_columns - matmul(near_terms[3], own_back)
    far_rows = -matmul(near_terms[4], own_back)
    top_share_map = jnp.where(
        is_bottom,
        jnp.concatenate([near_rows, far_rows], axis=0),
        jnp.concatenate([far_rows, near_rows], axis=0),
    )
    top_share_load = lax.dynamic_slice_in_dim(macro_load[:, :outer], start, share_size, 1) - matmul(
        near_terms[5], own_back
    )
    alpha_in = jnp.concatenate([macro_incoming[:, :share_size], macro_inside[:, :breadth]], axis=1)
    beta_in = jnp.concatenate([macro_incoming[:, share_size:], macro_inside[:, breadth:]], axis=1)
    alpha_value, beta_value = interface_values(level_terms, alpha_in, beta_in)
    role_values = jnp.where(
        is_alpha,
        jnp.concatenate([alpha_in, -beta_value], axis=1),
        jnp.concatenate([beta_in, -alpha_value], axis=1),
    )
    backward_table = jnp.stack(
        [
            block_index(canonical_blocks(ALPHA_ORDER[0]), breadth),
            block_index(canonical_blocks(ALPHA_ORDER[1]), breadth),
            block_index(canonical_blocks(BETA_ORDER[0]), breadth),
            block_index(canonical_blocks(BETA_ORDER[1]), breadth),
        ]
    )
    box_values = jnp.take(role_values, backward_table[role_index], axis=1)
    edge_values = matmul(box_values, own_edge) + own_edge_load
    return (
        top_share_map[None, None],
        top_share_load[None, None],
        box_values[None, None],
        edge_values[None, None],
    )


def solution(mesh):
    in_specs = (
        P("bx", "by", None, None),
        P("bx", "by", None, None),
        P("bx", "by", None),
        P("bx", "by", None, None),
        P("bx", "by", None, None),
        P("bx", "by", None, None),
    )
    out_specs = (
        P("bx", "by", None, None),
        P("bx", "by", None, None),
        P("bx", "by", None, None),
        P("bx", "by", None, None),
    )
    return jax.shard_map(body, mesh=mesh, in_specs=in_specs, out_specs=out_specs, check_vma=False)
```

profile of v0, /device:TPU:0, one launch (start us, length us, event | category | flops | bytes accessed | tf_op | source)
XLA Modules:
  0.0 114.0 jit_solution(9329707255149828205)
XLA Ops:
  1.1 0.7 copy-done.1
  1.8 1.9 %gather_fusion = s32[256]{0:T(256)S(1)} fusion(s32[256]{0:T(256)S(1)} %bitcast.135, s32[1024]{0:T(1024)S(1)} %pad_clamp_fusion.4), kind=kCustom, calls=%fused_computation.2 | custom fusion | bytes 3072 | tf_op jit(solution)/shard_map/jit(_take)/gather | solution.py:150
  3.8 1.0 gather_fusion.1
  4.9 1.0 gather_fusion.2
  6.1 3.0 %collective-permute-start = (f32[256,256]{1,0:T(8,128)S(1)}, f32[256,256]{1,0:T(8,128)S(1)}, u32[]{:S(2)}, u32[]{:S(2)}) collective-permute-start(f32[256,256]{1,0:T(8,128)S(1)} %select_bitcast_fusion.1), channel_id=1, source_target_pairs={{0,4},{4,0},{8,12},{12,8},{16,20},{20,16},{24,28},{28,24},{1,5},{5... | collective-permute-start | bytes 786440 | tf_op jit(solution)/shard_map/ppermute | solution.py:18
  9.2 0.7 gather_fusion.6
  10.1 0.8 collective-permute-start.3
  11.0 40.5 %psum.7 = f32[64]{0:T(128)S(1)} all-reduce(f32[64]{0:T(128)S(1)} %fusion.52), channel_id=1, replica_groups=mesh['bx'=8,'by'=4] {'bx','by'}, use_global_device_ids=true, to_apply=%region_5.7 | all-reduce | flops 64 | bytes 512 | tf_op jit(solution)/shard_map/psum | solution.py:134
  51.6 2.3 %collective-permute-start.5 = (f32[64,128]{1,0:T(8,128)S(1)}, f32[64,128]{1,0:T(8,128)S(1)}, u32[]{:S(2)}, u32[]{:S(2)}) collective-permute-start(f32[64,128]{1,0:T(8,128)S(1)} %bitcast_multiply_fusion), channel_id=1, source_target_pairs={{0,4},{4,0},{8,12},{12,8},{16,20},{20,16},{24,28},{28,24},{1,5},{5... | collective-permute-start | bytes 98312 | tf_op jit(solution)/shard_map/ppermute | solution.py:18
  54.1 1.6 %collective-permute-done.5 = f32[64,128]{1,0:T(8,128)S(1)} collective-permute-done((f32[64,128]{1,0:T(8,128)S(1)}, f32[64,128]{1,0:T(8,128)S(1)}, u32[]{:S(2)}, u32[]{:S(2)}) %collective-permute-start.5) | collective-permute-done | bytes 32800 | tf_op jit(solution)/shard_map/ppermute | solution.py:18
  56.8 5.8 %cholesky.31 = f32[64,64]{1,0:T(8,128)S(1)} custom-call(f32[64,64]{1,0:T(8,128)S(1)} %fusion.57), custom_call_target="Cholesky" | custom-call | tf_op jit(solution)/shard_map/jit(cholesky)/cholesky | solution.py:39
  62.7 0.6 compare_reduce_fusion.1
  63.3 0.7 fusion.50
  64.0 4.9 %custom-call.20 = f32[1,64,64]{1,2,0:T(8,128)S(1)} custom-call(f32[1,64,64]{2,1,0:T(8,128)S(1)} %fusion.50), custom_call_target="InvertDiagBlocksLowerTriangular" | custom-call | tf_op jit(solution)/shard_map/jit(_cho_solve)/triangular_solve | solution.py:40
  70.0 0.4 fusion.13
  71.7 0.4 convolution_subtract_fusion.2
  72.9 1.1 gather_fusion.5
  74.2 0.5 collective-permute-start.4
  75.6 1.7 %gather_fusion.3 = f32[384,384]{1,0:T(8,128)S(1)} fusion(f32[384,384]{1,0:T(8,128)S(1)} %maximum_maximum_fusion, s32[1024]{0:T(1024)S(1)} %pad_clamp_fusion.2), kind=kCustom, calls=%fused_computation.5 | custom fusion | bytes 1181184 | tf_op jit(solution)/shard_map/jit(_take)/gather | solution.py:164
  77.6 1.9 %gather_fusion.4 = f32[384,384]{1,0:T(8,128)S(1)} fusion(f32[384,384]{0,1:T(8,128)S(1)} %broadcast_select_fusion, s32[1024]{0:T(1024)S(1)} %pad_clamp_fusion.2), kind=kCustom, calls=%fused_computation.6 | custom fusion | bytes 1181184 | tf_op jit(solution)/shard_map/jit(_take)/gather | solution.py:164
  80.0 0.5 collective-permute-start.2
  80.7 0.5 collective-permute-done.1
  81.8 11.7 %cholesky.65 = f32[128,128]{1,0:T(8,128)S(1)} custom-call(f32[128,128]{1,0:T(8,128)S(1)} %fusion.24), custom_call_target="Cholesky" | custom-call | tf_op jit(solution)/shard_map/jit(cholesky)/cholesky | solution.py:39
  93.6 0.6 compare_reduce_fusion
  94.2 0.7 fusion.17
  94.9 9.8 %custom-call.21 = f32[1,128,128]{1,2,0:T(8,128)S(1)} custom-call(f32[1,128,128]{2,1,0:T(8,128)S(1)} %fusion.17), custom_call_target="InvertDiagBlocksLowerTriangular" | custom-call | tf_op jit(solution)/shard_map/jit(_cho_solve)/triangular_solve | solution.py:40
  106.1 0.6 slice-done
  106.7 0.8 fusion.9
  110.5 0.7 gather_fusion.7
  111.3 0.7 copy.35
  112.2 1.1 fusion.2
  113.3 0.7 maximum_select_fusion
  (125 shorter events, 12.5 us)
Async XLA Ops:
  0.6 3.1 %copy-start = (f32[1,1,256,256]{3,2,1,0:T(8,128)S(1)}, f32[1,1,256,256]{3,2,1,0:T(8,128)}, u32[]{:S(2)}) copy-start(f32[1,1,256,256]{3,2,1,0:T(8,128)} %param.8) | copy-start | bytes 786436
  1.1 0.7 copy-start.1
  6.0 3.1 %copy-start.5 = (f32[1,1,64,256]{3,2,1,0:T(8,128)S(1)}, f32[1,1,64,256]{3,2,1,0:T(8,128)}, u32[]{:S(2)}) copy-start(f32[1,1,64,256]{3,2,1,0:T(8,128)} %param.9) | copy-start | bytes 196612
  6.1 49.9 %collective-permute-start = (f32[256,256]{1,0:T(8,128)S(1)}, f32[256,256]{1,0:T(8,128)S(1)}, u32[]{:S(2)}, u32[]{:S(2)}) collective-permute-start(f32[256,256]{1,0:T(8,128)S(1)} %select_bitcast_fusion.1), channel_id=1, source_target_pairs={{0,4},{4,0},{8,12},{12,8},{16,20},{20,16},{24,28},{28,24},{1,5},{5... | collective-permute-start | bytes 786440 | tf_op jit(solution)/shard_map/ppermute | solution.py:18
  10.0 0.8 copy-start.3
  10.1 45.8 %collective-permute-start.3 = (f32[64,256]{1,0:T(8,128)S(1)}, f32[64,256]{1,0:T(8,128)S(1)}, u32[]{:S(2)}, u32[]{:S(2)}) collective-permute-start(f32[64,256]{1,0:T(8,128)S(1)} %select_bitcast_fusion.4), channel_id=1, source_target_pairs={{0,4},{4,0},{8,12},{12,8},{16,20},{20,16},{24,28},{28,24},{1,5},{5... | collective-permute-start | bytes 196616 | tf_op jit(solution)/shard_map/ppermute | solution.py:18
  51.6 4.2 %collective-permute-start.5 = (f32[64,128]{1,0:T(8,128)S(1)}, f32[64,128]{1,0:T(8,128)S(1)}, u32[]{:S(2)}, u32[]{:S(2)}) collective-permute-start(f32[64,128]{1,0:T(8,128)S(1)} %bitcast_multiply_fusion), channel_id=1, source_target_pairs={{0,4},{4,0},{8,12},{12,8},{16,20},{20,16},{24,28},{28,24},{1,5},{5... | collective-permute-start | bytes 98312 | tf_op jit(solution)/shard_map/ppermute | solution.py:18
  55.8 52.8 %collective-permute-start.6 = (f32[64,256]{1,0:T(8,128)S(1)}, f32[64,256]{1,0:T(8,128)S(1)}, u32[]{:S(2)}, u32[]{:S(2)}) collective-permute-start(f32[64,256]{1,0:T(8,128)S(1)} %pad_maximum_fusion.1), channel_id=1, source_target_pairs={{0,1},{1,0},{2,3},{3,2},{4,5},{5,4},{6,7},{7,6},{8,9},{9,8},{10,11... | collective-permute-start | bytes 196616 | tf_op jit(solution)/shard_map/ppermute | solution.py:18
  74.2 6.3 %copy-start.2 = (f32[64,384]{1,0:T(8,128)}, f32[64,384]{1,0:T(8,128)S(1)}, u32[]{:S(2)}) copy-start(f32[64,384]{1,0:T(8,128)S(1)} %select_bitcast_fusion.3) | copy-start | bytes 294916
  74.2 6.3 %collective-permute-start.4 = (f32[64,128]{1,0:T(8,128)S(1)}, f32[64,128]{1,0:T(8,128)S(1)}, u32[]{:S(2)}, u32[]{:S(2)}) collective-permute-start(f32[64,128]{1,0:T(8,128)S(1)} %slice.152), channel_id=1, source_target_pairs={{0,1},{1,0},{2,3},{3,2},{4,5},{5,4},{6,7},{7,6},{8,9},{9,8},{10,11... | collective-permute-start | bytes 98312 | tf_op jit(solution)/shard_map/ppermute | solution.py:18
  79.9 1.3 %collective-permute-start.1 = (f32[128,128]{1,0:T(8,128)S(1)}, f32[128,128]{1,0:T(8,128)S(1)}, u32[]{:S(2)}, u32[]{:S(2)}) collective-permute-start(f32[128,128]{1,0:T(8,128)S(1)} %slice.145), channel_id=1, source_target_pairs={{0,1},{1,0},{2,3},{3,2},{4,5},{5,4},{6,7},{7,6},{8,9},{9,8},{10,11... | collective-permute-start | bytes 196616 | tf_op jit(solution)/shard_map/ppermute | solution.py:18
  80.0 27.8 %collective-permute-start.2 = (f32[256,128]{1,0:T(8,128)S(1)}, f32[256,128]{1,0:T(8,128)S(1)}, u32[]{:S(2)}, u32[]{:S(2)}) collective-permute-start(f32[256,128]{1,0:T(8,128)S(1)} %slice.144), channel_id=1, source_target_pairs={{0,1},{1,0},{2,3},{3,2},{4,5},{5,4},{6,7},{7,6},{8,9},{9,8},{10,11... | collective-permute-start | bytes 393224 | tf_op jit(solution)/shard_map/ppermute | solution.py:18
  105.8 0.8 slice-start
  111.3 0.9 copy-start.4
  111.3 0.9 copy-start.6
where the time goes:
time: 114 us
  blocking collectives  40.5 us (36%)
  other arithmetic  37 us (32%)
  local copies, waits for them, and re-layouts  14 us (12%)
  matrix products  11.6 us (10%)
  starting transfers between devices  7.3 us (6%)
  waiting for transfers between devices  2.16 us (2%)
  between operations  1.44 us (1%)
    psum x1, blocking collectives, body(): power = lax.psum(jnp.sum(raw_incoming * raw_incoming, axis=1), ('bx', 'by'))  40.5 us
    another operation x6, other arithmetic, inverse_of(): factor = jnp.linalg.cholesky(normal_matrix)  18.9 us
    another operation x4, other arithmetic, inverse_of(): return jax.scipy.linalg.cho_solve((factor, True), kernel.T)  16 us
    dot_general x36, matrix products, matmul(): jnp.dot(first, second, precision=lax.Precision.HIGHEST, preferred_element...  10.7 us
    ppermute x7, starting transfers between devices, swapped(): return lax.ppermute(block, axis, route)  7.3 us
  transfers between devices with their start and end apart: 7, of which 2 were waited for; matrix products, arithmetic and copies ran while one was open for 45% of the time, Pallas kernels for 0%

commit v1 on v0

v1 whole, which is shorter than its diff:
```python
import functools

import jax
import jax.numpy as jnp
from jax import lax
from jax.experimental import pallas as pl
from jax.experimental.pallas import tpu as pltpu
from jax.sharding import PartitionSpec as P

VMEM = pl.BlockSpec(memory_space=pltpu.VMEM)
DOUBLINGS = 5


def swapped(block, axis, apart):
    count = lax.axis_size(axis)
    route = []
    for low in range(count):
        high = low | 1 << apart
        if high != low and high < count:
            route += [(low, high), (high, low)]
    return lax.ppermute(block, axis, route)


def dot(first, second):
    return jnp.dot(
        first, second, precision=lax.Precision.HIGH, preferred_element_type=jnp.float32
    )


def dot_one(first, second):
    return jnp.dot(first, second, preferred_element_type=jnp.float32)


def pieces(value):
    high = value.astype(jnp.bfloat16)
    rest = value - high.astype(jnp.float32)
    middle = rest.astype(jnp.bfloat16)
    low = (rest - middle.astype(jnp.float32)).astype(jnp.bfloat16)
    return high, middle, low


def own_parities():
    return lax.axis_index("bx") % 2, lax.axis_index("by") % 2


def permute_kernel(map_ref, load_ref, order_ref, incoming_ref, c0_ref, c1_ref, g0_ref, side_ref, power_ref):
    size = map_ref.shape[0]
    b = size // 4
    x_parity, y_parity = own_parities()
    order = order_ref[...]
    west, east, south, north = (order[:, n * b : (n + 1) * b] for n in range(4))
    outside = jnp.where(x_parity == 0, west, east)
    inside = jnp.where(x_parity == 0, east, west)
    first = jnp.where(y_parity == 0, south, north)
    second = jnp.where(y_parity == 0, north, south)
    picked = jnp.concatenate([outside, first, inside, second], axis=1)
    rows = lax.broadcasted_iota(jnp.int32, (size, size), 0)
    hot = jnp.where(rows == picked, 1.0, 0.0)
    hot_t = hot.T
    hot_rows = jnp.concatenate(
        [hot_t[: 2 * b], hot_t[3 * b :], hot_t[2 * b : 3 * b]], axis=0
    ).astype(jnp.bfloat16)
    hot = hot.astype(jnp.bfloat16)
    stacked = jnp.concatenate([map_ref[...], load_ref[...]], axis=0)
    by_column = [dot_one(piece, hot) for piece in pieces(stacked)]
    role_load = by_column[0][size:] + by_column[1][size:] + by_column[2][size:]
    by_row = [dot_one(hot_rows, part[:size].astype(jnp.bfloat16)) for part in by_column]
    role_map = by_row[0] + by_row[1] + by_row[2]
    c0_ref[...] = role_map[:, : 2 * b]
    c1_ref[...] = role_map[:, 2 * b :]
    g0_ref[...] = role_load[:, : 2 * b]
    count = load_ref.shape[0]
    raw = incoming_ref[...]
    side_ref[:count] = role_load[:, 2 * b :]
    side_ref[count:] = raw
    own_power = jnp.sum(raw * raw, axis=1, keepdims=True)
    at = lax.broadcasted_iota(jnp.int32, (count, 2 * b), 0)
    lane = lax.broadcasted_iota(jnp.int32, (count, 2 * b), 1)
    row = jnp.sum(jnp.where(at == lane, own_power, 0.0), axis=0, keepdims=True)
    power_ref[...] = jnp.broadcast_to(row, power_ref.shape)


def first_kernel(c0_ref, c1_ref, g0_ref, side_ref, f1_ref, fside_ref, p0_ref, send_ref, pl0_ref, z_ref):
    b = c0_ref.shape[1] // 2
    e = 3 * b
    count = g0_ref.shape[0]
    near, far = c1_ref[:, :b], f1_ref[:, :b]
    near_load, far_load = side_ref[:count], fside_ref[:count]
    a_cc, b_dd = near[e:], far[e:]
    both = dot(a_cc, f1_ref[e:])
    power = both[:, :b]
    right = jnp.concatenate([c0_ref[e:], c1_ref[e:, b:], both[:, b:]], axis=1)
    at = lax.broadcasted_iota(jnp.int32, (b, b), 0)
    lane = lax.broadcasted_iota(jnp.int32, (b, b), 1)
    z = jnp.where(at == lane, 1.0, 0.0) + power
    right = right + dot(power, right)
    for _ in range(DOUBLINGS - 1):
        power = dot(power, power)
        right = right + dot(power, right)
        z = z + dot(z, power)
    z_ref[...] = z
    back = dot(b_dd, right)
    t_part = jnp.concatenate(
        [back[:, :e], -(back[:, e:] + f1_ref[e:, b:])], axis=1
    )
    q_part = jnp.concatenate([-right[:, :e], right[:, e:]], axis=1)
    near_rows = dot(jnp.concatenate([near[:e], near_load[:, :b]], axis=0), t_part)
    far_rows = dot(jnp.concatenate([far[:e], far_load[:, :b]], axis=0), q_part)
    w = 2 * b
    p0_ref[:w] = near_rows[:w, :w] + c0_ref[:w]
    p0_ref[w : 2 * w] = far_rows[:w, :w]
    p0_ref[2 * w : 2 * w + b] = near_rows[w:e, :w] + c0_ref[w:e]
    p0_ref[2 * w + b : 3 * w] = far_rows[w:e, :w]
    near_y2 = jnp.concatenate([c1_ref[:e, b:], jnp.zeros((e, b), jnp.float32)], axis=1)
    far_y2 = jnp.concatenate([jnp.zeros((e, b), jnp.float32), f1_ref[:e, b:]], axis=1)
    send_ref[:w] = near_rows[:w, w:] + near_y2[:w]
    send_ref[w : 2 * w] = far_rows[:w, w:] + far_y2[:w]
    send_ref[2 * w : 2 * w + b] = near_rows[w:e, w:] + near_y2[w:]
    send_ref[2 * w + b : 3 * w] = far_rows[w:e, w:] + far_y2[w:]
    both_load = near_rows[e:] + far_rows[e:]
    pl0_ref[...] = g0_ref[...] + both_load[:, :w]
    send_ref[3 * w : 3 * w + count] = both_load[:, w:] + jnp.concatenate(
        [near_load[:, b:], far_load[:, b:]], axis=1
    )
    send_ref[3 * w + count : 3 * w + 2 * count] = side_ref[count:]
    send_ref[3 * w + 2 * count :] = fside_ref[count:]


def second_kernel(
    box_total, p0_ref, pl0_ref, own_ref, far_ref, c1_ref, f1_ref, side_ref, fside_ref, z_ref,
    power_ref, edge_ref, edge_load_ref, top_ref, top_load_ref, box_ref, values_ref
):
    w = p0_ref.shape[1]
    b = w // 2
    e = 3 * b
    count = pl0_ref.shape[0]
    x_parity, y_parity = own_parities()
    a_cc, b_dd = own_ref[2 * w : 3 * w], far_ref[2 * w : 3 * w]
    at = lax.broadcasted_iota(jnp.int32, (count, w), 0)
    lane = lax.broadcasted_iota(jnp.int32, (count, w), 1)
    total = jnp.sum(jnp.where(at == lane, power_ref[0:1], 0.0), axis=1, keepdims=True)
    factor = 1.0 / jnp.sqrt(total / (box_total * w) + 1e-06)
    near_inc = own_ref[3 * w + count : 3 * w + 2 * count] * factor
    next_inc = own_ref[3 * w + 2 * count : 3 * w + 3 * count] * factor
    far_incs = jnp.concatenate(
        [far_ref[3 * w + count : 3 * w + 2 * count], far_ref[3 * w + 2 * count : 3 * w + 3 * count]], axis=1
    ) * factor
    a_out = dot(jnp.concatenate([near_inc, next_inc], axis=1), own_ref[: 2 * w]) + own_ref[3 * w : 3 * w + count]
    b_out = dot(far_incs, far_ref[: 2 * w]) + far_ref[3 * w : 3 * w + count]
    left = b_out - dot(a_out, b_dd)
    power = dot(a_cc, b_dd)
    right = p0_ref[2 * w :]
    right = right + dot(power, right)
    left = left + dot(left, power)
    for _ in range(DOUBLINGS - 1):
        power = dot(power, power)
        right = right + dot(power, right)
        left = left + dot(left, power)
    back = dot(b_dd, right)
    near_rows = p0_ref[: 2 * w] + dot(own_ref[: 2 * w], back)
    far_rows = -dot(far_ref[: 2 * w], right)
    swap = x_parity
    near_at = pl.multiple_of(y_parity * 2 * w, w)
    far_at = pl.multiple_of((1 - y_parity) * 2 * w, w)
    top_ref[pl.ds(pl.multiple_of(near_at + swap * w, w), w)] = near_rows[:w]
    top_ref[pl.ds(pl.multiple_of(near_at + (1 - swap) * w, w), w)] = near_rows[w:]
    top_ref[pl.ds(pl.multiple_of(far_at + swap * w, w), w)] = far_rows[:w]
    top_ref[pl.ds(pl.multiple_of(far_at + (1 - swap) * w, w), w)] = far_rows[w:]
    top_load_ref[...] = (
        pl0_ref[...]
        + dot(own_ref[3 * w : 3 * w + count], back)
        - dot(far_ref[3 * w : 3 * w + count], right)
    )
    near_y2, next_y2 = -left[:, :b], -left[:, b:]
    near_in = jnp.concatenate([near_inc, near_y2], axis=1)
    next_in = jnp.concatenate([next_inc, next_y2], axis=1)
    a_out = dot(near_in, c1_ref[:e, :b]) + side_ref[:count, :b]
    b_out = dot(next_in, f1_ref[:e, :b]) + fside_ref[:count, :b]
    inside = -dot(b_out - dot(a_out, f1_ref[e:, :b]), z_ref[...])
    outside = near_inc[:, :b]
    first = near_inc[:, b:]
    x_sides = jnp.where(
        x_parity == 0,
        jnp.concatenate([outside, inside], axis=1),
        jnp.concatenate([inside, outside], axis=1),
    )
    y_sides = jnp.where(
        y_parity == 0,
        jnp.concatenate([first, near_y2], axis=1),
        jnp.concatenate([near_y2, first], axis=1),
    )
    box_ref[:, :w] = x_sides
    box_ref[:, w:] = y_sides
    values_ref[...] = dot(x_sides, edge_ref[:w]) + dot(y_sides, edge_ref[w:]) + edge_load_ref[...]


def call(kernel, outs, *operands):
    return pl.pallas_call(
        kernel,
        out_shape=[jax.ShapeDtypeStruct(shape, jnp.float32) for shape in outs],
        in_specs=[VMEM] * len(operands),
        out_specs=[VMEM] * len(outs),
    )(*operands)


def body(box_map, box_load, box_order, incoming, edge_map, edge_load):
    size = box_map.shape[2]
    w = size // 2
    b = size // 4
    count = box_load.shape[2]
    wide, high = lax.axis_size("bx"), lax.axis_size("by")
    c0, c1, g0, side, power = call(
        permute_kernel,
        [(size, w), (size, w), (count, w), (2 * count, w), (8, w)],
        box_map[0, 0], box_load[0, 0], box_order[0], incoming[0, 0],
    )
    for axis, extent in (("bx", wide), ("by", high)):
        for apart in range(1, extent.bit_length() - 1):
            power = power + swapped(power, axis, apart)
    power = power + swapped(power, "bx", 0)
    power = power + swapped(power, "by", 0)
    f1 = swapped(c1, "bx", 0)
    fside = swapped(side, "bx", 0)
    p0, send, pl0, z = call(
        first_kernel,
        [(3 * w, w), (3 * w + 3 * count, w), (count, w), (b, b)],
        c0, c1, g0, side, f1, fside,
    )
    far = swapped(send, "by", 0)
    top, top_load, box, values = call(
        functools.partial(second_kernel, wide * high),
        [(4 * w, w), (count, w), (count, size), (count, w)],
        p0, pl0, send, far, c1, f1, side, fside, z, power, edge_map[0, 0], edge_load[0, 0],
    )
    return top[None, None], top_load[None, None], box[None, None], values[None, None]


def solution(mesh):
    spec = P("bx", "by", None, None)
    return jax.shard_map(
        body,
        mesh=mesh,
        in_specs=(spec, spec, P("bx", "by", None), spec, spec, spec),
        out_specs=(spec,) * 4,
        check_vma=False,
    )
```

time: 114 us -> 37.7 us (0.33)
  blocking collectives: 40.5 us -> 0 us
  other arithmetic: 37 us -> 0.61 us
  local copies, waits for them, and re-layouts: 14 us -> 1.41 us
  matrix products: 11.6 us -> 0 us
  waiting for transfers between devices: 2.16 us -> 13.4 us
  Pallas kernels: 0 us -> 10.2 us
  starting transfers between devices: 7.3 us -> 11.3 us
    psum x1 -> x0, blocking collectives: 40.5 us -> none  [body(): power = lax.psum(jnp.sum(raw_incoming * raw_incoming, axis=1), ('bx', 'by'))]
    another operation x11 -> x0, other arithmetic: 34.9 us -> none  [the longest x6 18.9 us: inverse_of(): factor = jnp.linalg.cholesky(normal_matrix)]
    ppermute x7 -> x8, waiting for transfers between devices: 2.16 us -> 13.4 us  [swapped(): return lax.ppermute(block, axis, route)]
    gather x14 -> x0, local copies, waits for them, and re-layouts: 11 us -> none  [the longest x4 2.19 us: body(): role_map = jnp.take(jnp.take(own_map, picked, axis=0), picked, axis=1)]
    dot_general x36 -> x0, matrix products: 10.7 us -> none  [matmul(): jnp.dot(first, second, precision=lax.Precision.HIGHEST, preferred_element...]
    pallas_call x0 -> x3, Pallas kernels: none -> 10.2 us  [call(): pl.pallas_call(kernel, out_shape=[jax.ShapeDtypeStruct(shape, jnp.float32...]
    ppermute x7 -> x8, starting transfers between devices: 7.3 us -> 11.3 us  [swapped(): return lax.ppermute(block, axis, route)]
    select_n x15 -> x0, other arithmetic: 1.22 us -> none  [the longest x1 0.72 us: body(): jnp.where(is_bottom, jnp.concatenate([near_rows, far_rows], axis=0), jnp....]
  transfers between devices with their start and end apart: 7 -> 8, of which waited for: 2 -> 6; matrix products, arithmetic and copies ran while one was open for 45% -> 2% of each run, Pallas kernels for 0% -> 0%
where the time goes in v1:
time: 37.7 us; the launch traced here: 37.6 us
  waiting for transfers between devices  13.4 us (36%)
  starting transfers between devices  11.3 us (30%)
  Pallas kernels  10.2 us (27%)
  local copies, waits for them, and re-layouts  1.41 us (4%)
  between operations  0.65 us (2%)
  other arithmetic  0.61 us (2%)
    ppermute x8, waiting for transfers between devices, swapped(): return lax.ppermute(block, axis, route)  13.4 us
    ppermute x8, starting transfers between devices, swapped(): return lax.ppermute(block, axis, route)  11.3 us
    pallas_call x3, Pallas kernels, call(): pl.pallas_call(kernel, out_shape=[jax.ShapeDtypeStruct(shape, jnp.float32...  10.2 us
    unnamed x8, local copies, waits for them, and re-layouts  1.41 us
  transfers between devices with their start and end apart: 8, of which 6 were waited for; matrix products, arithmetic and copies ran while one was open for 2% of the time, Pallas kernels for 0%

profile of v1, /device:TPU:0, one launch (start us, length us, event | category | flops | bytes accessed | tf_op | source)
XLA Modules:
  0.0 37.6 jit_solution(5697804375767346121)
XLA Ops:
  0.6 2.5 %shard_map.93 = (f32[256,128]{1,0:T(8,128)}, f32[256,128]{1,0:T(8,128)}, f32[64,128]{1,0:T(8,128)}, f32[128,128]{1,0:T(8,128)}, f32[8,128]{1,0:T(8,128)}) custom-call(f32[256,256]{1,0:T(8,128)} %bitcast.10, f32[64,256]{1,0:T(8,128)} %bitcast.12, s32[1,256]{1,0:T(1,128)} %bitcast.15, f32[64,128]{1,0:T(8,128)} %bitcast.14), custom_call_target="tpu_custom_call" | custom-call | tf_op jit(solution)/shard_map/pallas_call | solution.py:198
  3.1 3.0 %collective-permute-start = (f32[256,128]{1,0:T(8,128)}, f32[256,128]{1,0:T(8,128)S(1)}, u32[]{:S(2)}, u32[]{:S(2)}) collective-permute-start(f32[256,128]{1,0:T(8,128)} %get-tuple-element.18.c1_ref), channel_id=1, source_target_pairs={{0,4},{4,0},{8,12},{12,8},{16,20},{20,16},{24,28},{28,24},{1,5},{5... | collective-permute-start | bytes 393224 | tf_op jit(solution)/shard_map/ppermute | solution.py:21
  6.1 0.0 collective-permute-start.1
  6.1 5.1 %collective-permute-done.1.fside_ref = f32[128,128]{1,0:T(8,128)S(1)} collective-permute-done((f32[128,128]{1,0:T(8,128)}, f32[128,128]{1,0:T(8,128)S(1)}, u32[]{:S(2)}, u32[]{:S(2)}) %collective-permute-start.1) | collective-permute-done | bytes 65568 | tf_op jit(solution)/shard_map/ppermute | solution.py:21
  11.2 0.0 copy-start.2
  11.2 0.0 collective-permute-done.f1_ref
  11.2 0.0 copy-start
  11.2 0.6 %copy-done.2 = f32[128,128]{1,0:T(8,128)} copy-done((f32[128,128]{1,0:T(8,128)}, f32[128,128]{1,0:T(8,128)S(1)}, u32[]{:S(2)}) %copy-start.2) | copy-done | bytes 65560
  11.8 0.1 copy-done
  11.9 0.0 copy-start.3
  11.9 3.4 %shard_map.94 = (f32[384,128]{1,0:T(8,128)}, f32[576,128]{1,0:T(8,128)}, f32[64,128]{1,0:T(8,128)}, f32[64,64]{1,0:T(8,128)}) custom-call(f32[256,128]{1,0:T(8,128)} %get-tuple-element.17.c0_ref, f32[256,128]{1,0:T(8,128)} %get-tuple-element.18.c1_ref, f32[64,128]{1,0:T(8,128)} %get-tuple-element.19.g0_ref, f32[128,128]{1,0:T(8,128)} %get-tuple-element.20.side_ref, ...), custom_call_target="tpu_custom_call" | custom-call | tf_op jit(solution)/shard_map/pallas_call | solution.py:198
  15.3 0.0 collective-permute-start.2
  15.3 0.0 copy-done.3
  15.3 1.9 %collective-permute-start.3 = (f32[8,128]{1,0:T(8,128)S(1)}, f32[8,128]{1,0:T(8,128)S(1)}, u32[]{:S(2)}, u32[]{:S(2)}) collective-permute-start(f32[8,128]{1,0:T(8,128)S(1)} %copy-done.3), channel_id=1, source_target_pairs={{0,8},{8,0},{4,12},{12,4},{16,24},{24,16},{20,28},{28,20},{1,9},{9... | collective-permute-start | bytes 12296 | tf_op jit(solution)/shard_map/ppermute | solution.py:21
  17.2 1.8 %collective-permute-done.3 = f32[8,128]{1,0:T(8,128)S(1)} collective-permute-done((f32[8,128]{1,0:T(8,128)S(1)}, f32[8,128]{1,0:T(8,128)S(1)}, u32[]{:S(2)}, u32[]{:S(2)}) %collective-permute-start.3) | collective-permute-done | bytes 4128 | tf_op jit(solution)/shard_map/ppermute | solution.py:21
  19.0 2.8 %collective-permute-start.4 = (f32[8,128]{1,0:T(8,128)S(1)}, f32[8,128]{1,0:T(8,128)S(1)}, u32[]{:S(2)}, u32[]{:S(2)}) collective-permute-start(f32[8,128]{1,0:T(8,128)S(1)} %add.15), channel_id=1, source_target_pairs={{0,16},{16,0},{4,20},{20,4},{8,24},{24,8},{12,28},{28,12},{1,17},{... | collective-permute-start | bytes 12296 | tf_op jit(solution)/shard_map/ppermute | solution.py:21
  21.9 1.7 %collective-permute-done.4 = f32[8,128]{1,0:T(8,128)S(1)} collective-permute-done((f32[8,128]{1,0:T(8,128)S(1)}, f32[8,128]{1,0:T(8,128)S(1)}, u32[]{:S(2)}, u32[]{:S(2)}) %collective-permute-start.4) | collective-permute-done | bytes 4128 | tf_op jit(solution)/shard_map/ppermute | solution.py:21
  23.5 1.8 %collective-permute-start.5 = (f32[8,128]{1,0:T(8,128)S(1)}, f32[8,128]{1,0:T(8,128)S(1)}, u32[]{:S(2)}, u32[]{:S(2)}) collective-permute-start(f32[8,128]{1,0:T(8,128)S(1)} %add.16), channel_id=1, source_target_pairs={{0,2},{2,0},{1,3},{3,1},{4,6},{6,4},{5,7},{7,5},{8,10},{10,8},{9,1... | collective-permute-start | bytes 12296 | tf_op jit(solution)/shard_map/ppermute | solution.py:21
  25.3 1.8 %collective-permute-done.5 = f32[8,128]{1,0:T(8,128)S(1)} collective-permute-done((f32[8,128]{1,0:T(8,128)S(1)}, f32[8,128]{1,0:T(8,128)S(1)}, u32[]{:S(2)}, u32[]{:S(2)}) %collective-permute-start.5) | collective-permute-done | bytes 4128 | tf_op jit(solution)/shard_map/ppermute | solution.py:21
  27.1 1.7 %collective-permute-start.6 = (f32[8,128]{1,0:T(8,128)S(1)}, f32[8,128]{1,0:T(8,128)S(1)}, u32[]{:S(2)}, u32[]{:S(2)}) collective-permute-start(f32[8,128]{1,0:T(8,128)S(1)} %add.17), channel_id=1, source_target_pairs={{0,4},{4,0},{8,12},{12,8},{16,20},{20,16},{24,28},{28,24},{1,5},{5... | collective-permute-start | bytes 12296 | tf_op jit(solution)/shard_map/ppermute | solution.py:21
  28.9 1.9 %collective-permute-done.6 = f32[8,128]{1,0:T(8,128)S(1)} collective-permute-done((f32[8,128]{1,0:T(8,128)S(1)}, f32[8,128]{1,0:T(8,128)S(1)}, u32[]{:S(2)}, u32[]{:S(2)}) %collective-permute-start.6) | collective-permute-done | bytes 4128 | tf_op jit(solution)/shard_map/ppermute | solution.py:21
  30.7 0.0 collective-permute-start.7
  30.8 1.2 %collective-permute-done.7 = f32[8,128]{1,0:T(8,128)S(1)} collective-permute-done((f32[8,128]{1,0:T(8,128)S(1)}, f32[8,128]{1,0:T(8,128)S(1)}, u32[]{:S(2)}, u32[]{:S(2)}) %collective-permute-start.7) | collective-permute-done | bytes 4128 | tf_op jit(solution)/shard_map/ppermute | solution.py:21
  31.9 0.6 %add.19.power_ref = f32[8,128]{1,0:T(8,128)} add(f32[8,128]{1,0:T(8,128)S(1)} %add.18, f32[8,128]{1,0:T(8,128)S(1)} %collective-permute-done.7) | non-fusion elementwise | flops 1024 | bytes 12288 | tf_op jit(solution)/shard_map/add | solution.py:221
  32.5 0.0 collective-permute-done.2.far_ref
  32.5 0.0 copy-start.1
  32.5 0.7 %copy-done.1 = f32[576,128]{1,0:T(8,128)} copy-done((f32[576,128]{1,0:T(8,128)}, f32[576,128]{1,0:T(8,128)S(1)}, u32[]{:S(2)}) %copy-start.1) | copy-done | bytes 294936
  33.2 4.3 %shard_map.95 = (f32[512,128]{1,0:T(8,128)}, f32[64,128]{1,0:T(8,128)}, f32[64,256]{1,0:T(8,128)}, f32[64,128]{1,0:T(8,128)}) custom-call(f32[384,128]{1,0:T(8,128)} %get-tuple-element.21.p0_ref, f32[64,128]{1,0:T(8,128)} %get-tuple-element.22.pl0_ref, f32[576,128]{1,0:T(8,128)} %get-tuple-element.23.own_ref, f32[576,128]{1,0:T(8,128)} %copy-done.1, ...), custom_call_target="tpu_custom_call" | custom-call | tf_op jit(solution)/shard_map/pallas_call | solution.py:198
  (4 shorter events, 0.0 us)
Async XLA Ops:
  3.1 8.1 %collective-permute-start = (f32[256,128]{1,0:T(8,128)}, f32[256,128]{1,0:T(8,128)S(1)}, u32[]{:S(2)}, u32[]{:S(2)}) collective-permute-start(f32[256,128]{1,0:T(8,128)} %get-tuple-element.18.c1_ref), channel_id=1, source_target_pairs={{0,4},{4,0},{8,12},{12,8},{16,20},{20,16},{24,28},{28,24},{1,5},{5... | collective-permute-start | bytes 393224 | tf_op jit(solution)/shard_map/ppermute | solution.py:21
  6.1 5.1 %collective-permute-start.1 = (f32[128,128]{1,0:T(8,128)}, f32[128,128]{1,0:T(8,128)S(1)}, u32[]{:S(2)}, u32[]{:S(2)}) collective-permute-start(f32[128,128]{1,0:T(8,128)} %get-tuple-element.20.side_ref), channel_id=1, source_target_pairs={{0,4},{4,0},{8,12},{12,8},{16,20},{20,16},{24,28},{28,24},{1,5},{5... | collective-permute-start | bytes 196616 | tf_op jit(solution)/shard_map/ppermute | solution.py:21
  11.2 0.6 %copy-start.2 = (f32[128,128]{1,0:T(8,128)}, f32[128,128]{1,0:T(8,128)S(1)}, u32[]{:S(2)}) copy-start(f32[128,128]{1,0:T(8,128)S(1)} %collective-permute-done.1.fside_ref) | copy-start | bytes 196612
  11.2 0.7 %copy-start = (f32[256,128]{1,0:T(8,128)}, f32[256,128]{1,0:T(8,128)S(1)}, u32[]{:S(2)}) copy-start(f32[256,128]{1,0:T(8,128)S(1)} %collective-permute-done.f1_ref) | copy-start | bytes 393220
  11.9 3.4 %copy-start.3 = (f32[8,128]{1,0:T(8,128)S(1)}, f32[8,128]{1,0:T(8,128)}, u32[]{:S(2)}) copy-start(f32[8,128]{1,0:T(8,128)} %get-tuple-element.25) | copy-start | bytes 12292
  15.3 17.2 %collective-permute-start.2 = (f32[576,128]{1,0:T(8,128)}, f32[576,128]{1,0:T(8,128)S(1)}, u32[]{:S(2)}, u32[]{:S(2)}) collective-permute-start(f32[576,128]{1,0:T(8,128)} %get-tuple-element.23.own_ref), channel_id=1, source_target_pairs={{0,1},{1,0},{2,3},{3,2},{4,5},{5,4},{6,7},{7,6},{8,9},{9,8},{10,11... | collective-permute-start | bytes 884744 | tf_op jit(solution)/shard_map/ppermute | solution.py:21
  15.3 3.7 %collective-permute-start.3 = (f32[8,128]{1,0:T(8,128)S(1)}, f32[8,128]{1,0:T(8,128)S(1)}, u32[]{:S(2)}, u32[]{:S(2)}) collective-permute-start(f32[8,128]{1,0:T(8,128)S(1)} %copy-done.3), channel_id=1, source_target_pairs={{0,8},{8,0},{4,12},{12,4},{16,24},{24,16},{20,28},{28,20},{1,9},{9... | collective-permute-start | bytes 12296 | tf_op jit(solution)/shard_map/ppermute | solution.py:21
  19.0 4.5 %collective-permute-start.4 = (f32[8,128]{1,0:T(8,128)S(1)}, f32[8,128]{1,0:T(8,128)S(1)}, u32[]{:S(2)}, u32[]{:S(2)}) collective-permute-start(f32[8,128]{1,0:T(8,128)S(1)} %add.15), channel_id=1, source_target_pairs={{0,16},{16,0},{4,20},{20,4},{8,24},{24,8},{12,28},{28,12},{1,17},{... | collective-permute-start | bytes 12296 | tf_op jit(solution)/shard_map/ppermute | solution.py:21
  23.5 3.6 %collective-permute-start.5 = (f32[8,128]{1,0:T(8,128)S(1)}, f32[8,128]{1,0:T(8,128)S(1)}, u32[]{:S(2)}, u32[]{:S(2)}) collective-permute-start(f32[8,128]{1,0:T(8,128)S(1)} %add.16), channel_id=1, source_target_pairs={{0,2},{2,0},{1,3},{3,1},{4,6},{6,4},{5,7},{7,5},{8,10},{10,8},{9,1... | collective-permute-start | bytes 12296 | tf_op jit(solution)/shard_map/ppermute | solution.py:21
  27.1 3.6 %collective-permute-start.6 = (f32[8,128]{1,0:T(8,128)S(1)}, f32[8,128]{1,0:T(8,128)S(1)}, u32[]{:S(2)}, u32[]{:S(2)}) collective-permute-start(f32[8,128]{1,0:T(8,128)S(1)} %add.17), channel_id=1, source_target_pairs={{0,4},{4,0},{8,12},{12,8},{16,20},{20,16},{24,28},{28,24},{1,5},{5... | collective-permute-start | bytes 12296 | tf_op jit(solution)/shard_map/ppermute | solution.py:21
  30.7 1.2 %collective-permute-start.7 = (f32[8,128]{1,0:T(8,128)S(1)}, f32[8,128]{1,0:T(8,128)S(1)}, u32[]{:S(2)}, u32[]{:S(2)}) collective-permute-start(f32[8,128]{1,0:T(8,128)S(1)} %add.18), channel_id=1, source_target_pairs={{0,1},{1,0},{2,3},{3,2},{4,5},{5,4},{6,7},{7,6},{8,9},{9,8},{10,11... | collective-permute-start | bytes 12296 | tf_op jit(solution)/shard_map/ppermute | solution.py:21
  32.5 0.7 %copy-start.1 = (f32[576,128]{1,0:T(8,128)}, f32[576,128]{1,0:T(8,128)S(1)}, u32[]{:S(2)}) copy-start(f32[576,128]{1,0:T(8,128)S(1)} %collective-permute-done.2.far_ref) | copy-start | bytes 884740

commit v2 on v1

v2 whole, which is shorter than its diff:
```python
import functools

import jax
import jax.numpy as jnp
from jax import lax
from jax.experimental import pallas as pl
from jax.experimental.pallas import tpu as pltpu
from jax.sharding import PartitionSpec as P


VMEM = pl.BlockSpec(memory_space=pltpu.VMEM)
DOUBLINGS = 5


def swapped(block, axis, apart):
    count = lax.axis_size(axis)
    route = []
    for low in range(count):
        high = low | 1 << apart
        if high != low and high < count:
            route += [(low, high), (high, low)]
    return lax.ppermute(block, axis, route)


def dot(first, second):
    return jnp.dot(
        first, second, precision=lax.Precision.HIGH, preferred_element_type=jnp.float32
    )


def dot_one(first, second):
    return jnp.dot(first, second, preferred_element_type=jnp.float32)


def pieces(value):
    high = value.astype(jnp.bfloat16)
    rest = value - high.astype(jnp.float32)
    middle = rest.astype(jnp.bfloat16)
    low = (rest - middle.astype(jnp.float32)).astype(jnp.bfloat16)
    return high, middle, low


def own_parities():
    return lax.axis_index("bx") % 2, lax.axis_index("by") % 2


def permute_kernel(map_ref, load_ref, order_ref, c0_ref, c1_ref, g0_ref, g1_ref, all_ref, own_order_ref, sems):
    size = map_ref.shape[0]
    b = size // 4
    x_parity, y_parity = own_parities()
    order_copy = pltpu.make_async_copy(order_ref, own_order_ref, sems.at[0])
    map_copy = pltpu.make_async_copy(map_ref, all_ref.at[:size], sems.at[1])
    load_copy = pltpu.make_async_copy(load_ref, all_ref.at[size:], sems.at[2])
    for copy in (order_copy, map_copy, load_copy):
        copy.start()
    order_copy.wait()
    order = own_order_ref[...]
    west, east, south, north = (order[:, n * b : (n + 1) * b] for n in range(4))
    outside = jnp.where(x_parity == 0, west, east)
    inside = jnp.where(x_parity == 0, east, west)
    first = jnp.where(y_parity == 0, south, north)
    second = jnp.where(y_parity == 0, north, south)
    picked = jnp.concatenate([outside, first, inside, second], axis=1)
    rows = lax.broadcasted_iota(jnp.int32, (size, size), 0)
    hot = jnp.where(rows == picked, 1.0, 0.0)
    hot_t = hot.T
    hot_rows = jnp.concatenate(
        [hot_t[: 2 * b], hot_t[3 * b :], hot_t[2 * b : 3 * b]], axis=0
    ).astype(jnp.bfloat16)
    hot = hot.astype(jnp.bfloat16)
    map_copy.wait()
    load_copy.wait()
    by_column = [dot_one(piece, hot) for piece in pieces(all_ref[...])]
    role_load = by_column[0][size:] + by_column[1][size:] + by_column[2][size:]
    by_row = [dot_one(hot_rows, part[:size].astype(jnp.bfloat16)) for part in by_column]
    role_map = by_row[0] + by_row[1] + by_row[2]
    c0_ref[...] = role_map[:, : 2 * b]
    c1_ref[...] = role_map[:, 2 * b :]
    g0_ref[...] = role_load[:, : 2 * b]
    g1_ref[...] = role_load[:, 2 * b :]


def pair_power_kernel(inc_ref, next_ref, power_ref):
    count, w = inc_ref.shape
    own, other = inc_ref[...], next_ref[...]
    total = jnp.sum(own * own + other * other, axis=1, keepdims=True)
    at = lax.broadcasted_iota(jnp.int32, (count, w), 0)
    lane = lax.broadcasted_iota(jnp.int32, (count, w), 1)
    row = jnp.sum(jnp.where(at == lane, total, 0.0), axis=0, keepdims=True)
    power_ref[...] = jnp.broadcast_to(row, power_ref.shape)


def first_solve_kernel(c0_ref, c1_ref, f1_ref, t_ref, q_ref, z_ref):
    b = c0_ref.shape[1] // 2
    e = 3 * b
    a_cc, b_dd = c1_ref[e:, :b], f1_ref[e:, :b]
    both = dot(a_cc, f1_ref[e:])
    power = both[:, :b]
    right = jnp.concatenate([c0_ref[e:], c1_ref[e:, b:], both[:, b:]], axis=1)
    at = lax.broadcasted_iota(jnp.int32, (b, b), 0)
    lane = lax.broadcasted_iota(jnp.int32, (b, b), 1)
    z = jnp.where(at == lane, 1.0, 0.0) + power
    right = right + dot(power, right)
    for _ in range(DOUBLINGS - 1):
        power = dot(power, power)
        right = right + dot(power, right)
        z = z + dot(z, power)
    z_ref[...] = z
    back = dot(b_dd, right)
    t_ref[...] = jnp.concatenate([back[:, :e], -(back[:, e:] + f1_ref[e:, b:])], axis=1)
    q_ref[...] = jnp.concatenate([-right[:, :e], right[:, e:]], axis=1)


def first_merge_kernel(
    c0_ref, c1_ref, g0_ref, g1_ref, f1_ref, fg1_ref, inc_ref, next_ref, t_ref, q_ref,
    p0_ref, pl0_ref, send_ref
):
    w = c0_ref.shape[1]
    b = w // 2
    e = 3 * b
    count = g0_ref.shape[0]
    near_rows = dot(jnp.concatenate([c1_ref[:e, :b], g1_ref[:, :b]], axis=0), t_ref[...])
    far_rows = dot(jnp.concatenate([f1_ref[:e, :b], fg1_ref[:, :b]], axis=0), q_ref[...])
    p0_ref[:w] = near_rows[:w, :w] + c0_ref[:w]
    p0_ref[w : 2 * w] = far_rows[:w, :w]
    p0_ref[2 * w : 2 * w + b] = near_rows[w:e, :w] + c0_ref[w:e]
    p0_ref[2 * w + b :] = far_rows[w:e, :w]
    near_y2 = jnp.concatenate([c1_ref[:e, b:], jnp.zeros((e, b), jnp.float32)], axis=1)
    far_y2 = jnp.concatenate([jnp.zeros((e, b), jnp.float32), f1_ref[:e, b:]], axis=1)
    send_ref[:w] = near_rows[:w, w:] + near_y2[:w]
    send_ref[w : 2 * w] = far_rows[:w, w:] + far_y2[:w]
    send_ref[2 * w : 2 * w + b] = near_rows[w:e, w:] + near_y2[w:]
    send_ref[2 * w + b : 3 * w] = far_rows[w:e, w:] + far_y2[w:]
    both_load = near_rows[e:] + far_rows[e:]
    pl0_ref[...] = g0_ref[...] + both_load[:, :w]
    send_ref[3 * w : 3 * w + count] = both_load[:, w:] + jnp.concatenate(
        [g1_ref[:, b:], fg1_ref[:, b:]], axis=1
    )
    send_ref[3 * w + count : 3 * w + 2 * count] = inc_ref[...]
    send_ref[3 * w + 2 * count :] = next_ref[...]


def second_solve_kernel(p0_ref, own_ref, far_ref, right_ref, back_ref, left_ref):
    w = p0_ref.shape[1]
    count = (own_ref.shape[0] - 3 * w) // 3
    a_cc, b_dd = own_ref[2 * w : 3 * w], far_ref[2 * w : 3 * w]
    at = 3 * w + count
    own_incs = jnp.concatenate([own_ref[at : at + count], own_ref[at + count :]], axis=1)
    far_incs = jnp.concatenate([far_ref[at : at + count], far_ref[at + count :]], axis=1)
    a_out = jnp.concatenate([dot(own_incs, own_ref[: 2 * w]), own_ref[3 * w : at]], axis=0)
    b_out = jnp.concatenate([dot(far_incs, far_ref[: 2 * w]), far_ref[3 * w : at]], axis=0)
    left = b_out - dot(a_out, b_dd)
    power = dot(a_cc, b_dd)
    right = p0_ref[2 * w :]
    right = right + dot(power, right)
    left = left + dot(left, power)
    for _ in range(DOUBLINGS - 1):
        power = dot(power, power)
        right = right + dot(power, right)
        left = left + dot(left, power)
    right_ref[...] = right
    back_ref[...] = dot(b_dd, right)
    left_ref[...] = -left


def second_merge_kernel(
    p0_ref, pl0_ref, own_ref, far_ref, c1_ref, g1_ref, f1_ref, fg1_ref, inc_ref, next_ref, z_ref,
    right_ref, back_ref, left_ref, edge_ref, edge_load_ref, top_ref, top_load_ref, box_ref, values_ref,
    own_edge_ref, own_edge_load_ref, own_top_ref, own_top_load_ref, sems
):
    edge_copy = pltpu.make_async_copy(edge_ref, own_edge_ref, sems.at[0])
    edge_load_copy = pltpu.make_async_copy(edge_load_ref, own_edge_load_ref, sems.at[1])
    edge_copy.start()
    edge_load_copy.start()
    w = p0_ref.shape[1]
    b = w // 2
    e = 3 * b
    count = pl0_ref.shape[0]
    x_parity, y_parity = own_parities()
    near_rows = p0_ref[: 2 * w] + dot(own_ref[: 2 * w], back_ref[...])
    far_rows = -dot(far_ref[: 2 * w], right_ref[...])
    near_at = y_parity * 2 * w
    far_at = (1 - y_parity) * 2 * w
    for rows, start in ((near_rows, near_at), (far_rows, far_at)):
        own_top_ref[pl.ds(pl.multiple_of(start + x_parity * w, w), w)] = rows[:w]
        own_top_ref[pl.ds(pl.multiple_of(start + (1 - x_parity) * w, w), w)] = rows[w:]
    own_top_load_ref[...] = (
        pl0_ref[...]
        + dot(own_ref[3 * w : 3 * w + count], back_ref[...])
        - dot(far_ref[3 * w : 3 * w + count], right_ref[...])
    )
    top_copy = pltpu.make_async_copy(own_top_ref, top_ref, sems.at[2])
    top_load_copy = pltpu.make_async_copy(own_top_load_ref, top_load_ref, sems.at[3])
    top_copy.start()
    top_load_copy.start()
    none = jnp.zeros((count, w), jnp.float32)
    near_inc = jnp.concatenate([inc_ref[...], none], axis=0)
    next_inc = jnp.concatenate([next_ref[...], none], axis=0)
    near_y2 = left_ref[:, :b]
    near_in = jnp.concatenate([near_inc, near_y2], axis=1)
    next_in = jnp.concatenate([next_inc, left_ref[:, b:]], axis=1)
    a_out = dot(near_in, c1_ref[:e, :b]) + jnp.concatenate([none[:, :b], g1_ref[:, :b]], axis=0)
    b_out = dot(next_in, f1_ref[:e, :b]) + jnp.concatenate([none[:, :b], fg1_ref[:, :b]], axis=0)
    inside = -dot(b_out - dot(a_out, f1_ref[e:, :b]), z_ref[...])
    outside = near_inc[:, :b]
    first = near_inc[:, b:]
    x_sides = jnp.where(
        x_parity == 0,
        jnp.concatenate([outside, inside], axis=1),
        jnp.concatenate([inside, outside], axis=1),
    )
    y_sides = jnp.where(
        y_parity == 0,
        jnp.concatenate([first, near_y2], axis=1),
        jnp.concatenate([near_y2, first], axis=1),
    )
    box_ref[:, :w] = x_sides
    box_ref[:, w:] = y_sides
    edge_copy.wait()
    edge_load_copy.wait()
    values = dot(x_sides, own_edge_ref[:w]) + dot(y_sides, own_edge_ref[w:])
    values_ref[:count] = values[:count]
    values_ref[count:] = values[count:] + own_edge_load_ref[...]
    top_copy.wait()
    top_load_copy.wait()


def scale_kernel(box_total, box_ref, values_ref, power_ref, added_ref, out_box_ref, out_values_ref):
    count, w = out_values_ref.shape
    at = lax.broadcasted_iota(jnp.int32, (count, w), 0)
    lane = lax.broadcasted_iota(jnp.int32, (count, w), 1)
    power = power_ref[0:1] + added_ref[0:1]
    total = jnp.sum(jnp.where(at == lane, power, 0.0), axis=1, keepdims=True)
    factor = 1.0 / jnp.sqrt(total / (box_total * w) + 1e-06)
    out_box_ref[...] = box_ref[:count] * factor + box_ref[count:]
    out_values_ref[...] = values_ref[:count] * factor + values_ref[count:]


def call(kernel, outs, *operands, distant=(), scratch=()):
    away = pl.BlockSpec(memory_space=pl.ANY)
    placed = [
        operand if number in distant else pltpu.with_memory_space_constraint(operand, pltpu.VMEM)
        for number, operand in enumerate(operands)
    ]
    return pl.pallas_call(
        kernel,
        out_shape=[
            (pltpu.VMEM if place == "here" else pltpu.HBM)(shape, jnp.float32)
            for place, shape in outs
        ],
        in_specs=[away if number in distant else VMEM for number in range(len(operands))],
        out_specs=[away if place == "copied" else VMEM for place, shape in outs],
        scratch_shapes=list(scratch),
    )(*placed)


def body(box_map, box_load, box_order, incoming, edge_map, edge_load):
    size = box_map.shape[2]
    w = size // 2
    b = size // 4
    count = box_load.shape[2]
    wide, high = lax.axis_size("bx"), lax.axis_size("by")
    here, there, copied = "here", "there", "copied"
    own_inc = incoming[0, 0]
    next_inc = swapped(own_inc, "bx", 0)
    c0, c1, g0, g1 = call(
        permute_kernel,
        [(here, (size, w)), (here, (size, w)), (here, (count, w)), (here, (count, w))],
        box_map[0, 0], box_load[0, 0], box_order[0],
        distant=(0, 1, 2),
        scratch=[
            pltpu.VMEM((size + count, size), jnp.float32),
            pltpu.VMEM((1, size), jnp.int32),
            pltpu.SemaphoreType.DMA((3,)),
        ],
    )
    f1 = swapped(c1, "bx", 0)
    (power,) = call(pair_power_kernel, [(here, (8, w))], own_inc, next_inc)
    stages = [("by", apart) for apart in range(1, high.bit_length() - 1)]
    stages += [("bx", apart) for apart in range(1, wide.bit_length() - 1)]
    for axis, apart in stages:
        power = power + swapped(power, axis, apart)
    fg1 = swapped(g1, "bx", 0)
    added = swapped(power, "by", 0)
    t_part, q_part, z = call(
        first_solve_kernel,
        [(here, (b, size)), (here, (b, size)), (here, (b, b))],
        c0, c1, f1,
    )
    p0, pl0, own = call(
        first_merge_kernel,
        [(here, (3 * w, w)), (here, (count, w)), (here, (3 * w + 3 * count, w))],
        c0, c1, g0, g1, f1, fg1, own_inc, next_inc, t_part, q_part,
    )
    far = swapped(own, "by", 0)
    right, back, left = call(
        second_solve_kernel,
        [(here, (w, w)), (here, (w, w)), (here, (2 * count, w))],
        p0, own, far,
    )
    top, top_load, box, values = call(
        second_merge_kernel,
        [(copied, (4 * w, w)), (copied, (count, w)), (here, (2 * count, size)), (here, (2 * count, w))],
        p0, pl0, own, far, c1, g1, f1, fg1, own_inc, next_inc, z, right, back, left,
        edge_map[0, 0], edge_load[0, 0],
        distant=(14, 15),
        scratch=[
            pltpu.VMEM((size, w), jnp.float32),
            pltpu.VMEM((count, w), jnp.float32),
            pltpu.VMEM((4 * w, w), jnp.float32),
            pltpu.VMEM((count, w), jnp.float32),
            pltpu.SemaphoreType.DMA((4,)),
        ],
    )
    box, values = call(
        functools.partial(scale_kernel, wide * high),
        [(there, (count, size)), (there, (count, w))],
        box, values, power, added,
    )
    return top[None, None], top_load[None, None], box[None, None], values[None, None]


def solution(mesh):
    spec = P("bx", "by", None, None)

    return jax.shard_map(
        body,
        mesh=mesh,
        in_specs=(spec, spec, P("bx", "by", None), spec, spec, spec),
        out_specs=(spec,) * 4,
        check_vma=False,
    )
```

time: 37.7 us -> 26.9 us (0.71)
  waiting for transfers between devices: 13.4 us -> 7.47 us
  Pallas kernels: 10.2 us -> 6.9 us
  local copies, waits for them, and re-layouts: 1.41 us -> 0.01 us
  other arithmetic: 0.61 us -> 0.01 us
    ppermute x8, waiting for transfers between devices: 13.4 us -> 7.47 us  [swapped(): return lax.ppermute(block, axis, route)]
    pallas_call x3 -> x7, Pallas kernels: 10.2 us -> 6.9 us  [call(): pl.pallas_call(kernel, out_shape=[(pltpu.VMEM if place == 'here' else plt...]
    unnamed x8 -> x2, local copies, waits for them, and re-layouts: 1.41 us -> 0.01 us
    add x2 -> x0, other arithmetic: 0.6 us -> none  [the longest x1 0.59 us: body(): power = power + swapped(power, 'by', 0)]
  transfers between devices with their start and end apart: 8 -> 8, of which waited for: 6 -> 4; matrix products, arithmetic and copies ran while one was open for 2% -> 0% of each run, Pallas kernels for 0% -> 16%
where the time goes in v2:
time: 26.9 us; the launch traced here: 26.7 us
  starting transfers between devices  11.6 us (43%)
  waiting for transfers between devices  7.47 us (28%)
  Pallas kernels  6.9 us (26%)
  between operations  0.71 us (3%)
    ppermute x8, starting transfers between devices, swapped(): return lax.ppermute(block, axis, route)  11.6 us
    ppermute x8, waiting for transfers between devices, swapped(): return lax.ppermute(block, axis, route)  7.47 us
    pallas_call x7, Pallas kernels, call(): pl.pallas_call(kernel, out_shape=[(pltpu.VMEM if place == 'here' else plt...  6.9 us
  transfers between devices with their start and end apart: 8, of which 4 were waited for; matrix products, arithmetic and copies ran while one was open for 0% of the time, Pallas kernels for 16%

profile of v2, /device:TPU:0, one launch (start us, length us, event | category | flops | bytes accessed | tf_op | source)
XLA Modules:
  0.0 26.7 jit_solution(5196701077372538052)
XLA Ops:
  0.6 0.0 copy-start
  0.6 1.6 %shard_map.93 = (f32[256,128]{1,0:T(8,128)S(1)}, f32[256,128]{1,0:T(8,128)S(1)}, f32[64,128]{1,0:T(8,128)S(1)}, f32[64,128]{1,0:T(8,128)S(1)}) custom-call(f32[256,256]{1,0:T(8,128)} %bitcast.14, f32[64,256]{1,0:T(8,128)} %bitcast.16, s32[1,256]{1,0:T(1,128)} %bitcast.18), custom_call_target="tpu_custom_call" | custom-call | tf_op jit(solution)/shard_map/pallas_call | solution.py:245
  2.3 3.0 %collective-permute-start = (f32[256,128]{1,0:T(8,128)S(1)}, f32[256,128]{1,0:T(8,128)S(1)}, u32[]{:S(2)}, u32[]{:S(2)}) collective-permute-start(f32[256,128]{1,0:T(8,128)S(1)} %get-tuple-element.24.c1_ref), channel_id=1, source_target_pairs={{0,4},{4,0},{8,12},{12,8},{16,20},{20,16},{24,28},{28,24},{1,5},{5... | collective-permute-start | bytes 393224 | tf_op jit(solution)/shard_map/ppermute | solution.py:22
  5.3 0.1 collective-permute-start.1
  5.4 0.0 copy-done
  5.4 1.9 %collective-permute-start.2 = (f32[64,128]{1,0:T(8,128)S(1)}, f32[64,128]{1,0:T(8,128)S(1)}, u32[]{:S(2)}, u32[]{:S(2)}) collective-permute-start(f32[64,128]{1,0:T(8,128)S(1)} %bitcast.10), channel_id=1, source_target_pairs={{0,4},{4,0},{8,12},{12,8},{16,20},{20,16},{24,28},{28,24},{1,5},{5... | collective-permute-start | bytes 98312 | tf_op jit(solution)/shard_map/ppermute | solution.py:22
  7.3 2.2 %collective-permute-done.f1_ref = f32[256,128]{1,0:T(8,128)S(1)} collective-permute-done((f32[256,128]{1,0:T(8,128)S(1)}, f32[256,128]{1,0:T(8,128)S(1)}, u32[]{:S(2)}, u32[]{:S(2)}) %collective-permute-start) | collective-permute-done | bytes 131104 | tf_op jit(solution)/shard_map/ppermute | solution.py:22
  9.5 1.2 %shard_map.94 = (f32[64,256]{1,0:T(8,128)S(1)}, f32[64,256]{1,0:T(8,128)S(1)}, f32[64,64]{1,0:T(8,128)S(1)}) custom-call(f32[256,128]{1,0:T(8,128)S(1)} %get-tuple-element.23.c0_ref, f32[256,128]{1,0:T(8,128)S(1)} %get-tuple-element.24.c1_ref, f32[256,128]{1,0:T(8,128)S(1)} %collective-permute-done.f1_ref), custom_call_target="tpu_custom_call" | custom-call | tf_op jit(solution)/shard_map/pallas_call | solution.py:245
  10.7 0.0 collective-permute-done.1.fg1_ref
  10.7 0.0 collective-permute-done.2.next_ref
  10.7 0.4 %shard_map.95 = (f32[384,128]{1,0:T(8,128)S(1)}, f32[64,128]{1,0:T(8,128)S(1)}, f32[576,128]{1,0:T(8,128)S(1)}) custom-call(f32[256,128]{1,0:T(8,128)S(1)} %get-tuple-element.23.c0_ref, f32[256,128]{1,0:T(8,128)S(1)} %get-tuple-element.24.c1_ref, f32[64,128]{1,0:T(8,128)S(1)} %get-tuple-element.25.g0_ref, f32[64,128]{1,0:T(8,128)S(1)} %get-tuple-element.26.g1_ref, ...), custom_call_target="tpu_custom_call" | custom-call | tf_op jit(solution)/shard_map/pallas_call | solution.py:245
  11.1 0.1 collective-permute-start.3
  11.2 0.1 shard_map.98
  11.3 1.8 %collective-permute-start.4 = (f32[8,128]{1,0:T(8,128)S(1)}, f32[8,128]{1,0:T(8,128)S(1)}, u32[]{:S(2)}, u32[]{:S(2)}) collective-permute-start(f32[8,128]{1,0:T(8,128)S(1)} %shard_map.98), channel_id=1, source_target_pairs={{0,2},{2,0},{1,3},{3,1},{4,6},{6,4},{5,7},{7,5},{8,10},{10,8},{9,1... | collective-permute-start | bytes 12296 | tf_op jit(solution)/shard_map/ppermute | solution.py:22
  13.1 1.8 %collective-permute-done.4 = f32[8,128]{1,0:T(8,128)S(1)} collective-permute-done((f32[8,128]{1,0:T(8,128)S(1)}, f32[8,128]{1,0:T(8,128)S(1)}, u32[]{:S(2)}, u32[]{:S(2)}) %collective-permute-start.4) | collective-permute-done | bytes 4128 | tf_op jit(solution)/shard_map/ppermute | solution.py:22
  14.9 1.8 %collective-permute-start.5 = (f32[8,128]{1,0:T(8,128)S(1)}, f32[8,128]{1,0:T(8,128)S(1)}, u32[]{:S(2)}, u32[]{:S(2)}) collective-permute-start(f32[8,128]{1,0:T(8,128)S(1)} %add.9), channel_id=1, source_target_pairs={{0,8},{8,0},{4,12},{12,4},{16,24},{24,16},{20,28},{28,20},{1,9},{9... | collective-permute-start | bytes 12296 | tf_op jit(solution)/shard_map/ppermute | solution.py:22
  16.8 1.8 %collective-permute-done.5 = f32[8,128]{1,0:T(8,128)S(1)} collective-permute-done((f32[8,128]{1,0:T(8,128)S(1)}, f32[8,128]{1,0:T(8,128)S(1)}, u32[]{:S(2)}, u32[]{:S(2)}) %collective-permute-start.5) | collective-permute-done | bytes 4128 | tf_op jit(solution)/shard_map/ppermute | solution.py:22
  18.5 2.8 %collective-permute-start.6 = (f32[8,128]{1,0:T(8,128)S(1)}, f32[8,128]{1,0:T(8,128)S(1)}, u32[]{:S(2)}, u32[]{:S(2)}) collective-permute-start(f32[8,128]{1,0:T(8,128)S(1)} %add.10), channel_id=1, source_target_pairs={{0,16},{16,0},{4,20},{20,4},{8,24},{24,8},{12,28},{28,12},{1,17},{... | collective-permute-start | bytes 12296 | tf_op jit(solution)/shard_map/ppermute | solution.py:22
  21.4 1.7 %collective-permute-done.6 = f32[8,128]{1,0:T(8,128)S(1)} collective-permute-done((f32[8,128]{1,0:T(8,128)S(1)}, f32[8,128]{1,0:T(8,128)S(1)}, u32[]{:S(2)}, u32[]{:S(2)}) %collective-permute-start.6) | collective-permute-done | bytes 4128 | tf_op jit(solution)/shard_map/ppermute | solution.py:22
  23.1 0.0 collective-permute-start.7
  23.1 0.0 collective-permute-done.3.far_ref
  23.1 1.4 %shard_map.96 = (f32[128,128]{1,0:T(8,128)S(1)}, f32[128,128]{1,0:T(8,128)S(1)}, f32[128,128]{1,0:T(8,128)S(1)}) custom-call(f32[384,128]{1,0:T(8,128)S(1)} %get-tuple-element.29.p0_ref, f32[576,128]{1,0:T(8,128)S(1)} %get-tuple-element.31.own_ref, f32[576,128]{1,0:T(8,128)S(1)} %collective-permute-done.3.far_ref), custom_call_target="tpu_custom_call" | custom-call | tf_op jit(solution)/shard_map/pallas_call | solution.py:245
  24.5 1.5 %shard_map.97 = (f32[512,128]{1,0:T(8,128)}, f32[64,128]{1,0:T(8,128)}, f32[128,256]{1,0:T(8,128)S(1)}, f32[128,128]{1,0:T(8,128)S(1)}) custom-call(f32[384,128]{1,0:T(8,128)S(1)} %get-tuple-element.29.p0_ref, f32[64,128]{1,0:T(8,128)S(1)} %get-tuple-element.30.pl0_ref, f32[576,128]{1,0:T(8,128)S(1)} %get-tuple-element.31.own_ref, ...), custom_call_target="tpu_custom_call" | custom-call | tf_op jit(solution)/shard_map/pallas_call | solution.py:245
  26.0 0.0 collective-permute-done.7.added_ref
  26.0 0.7 %shard_map.99 = (f32[64,256]{1,0:T(8,128)}, f32[64,128]{1,0:T(8,128)}) custom-call(f32[128,256]{1,0:T(8,128)S(1)} %get-tuple-element.38.box_ref, f32[128,128]{1,0:T(8,128)S(1)} %get-tuple-element.39.values_ref, f32[8,128]{1,0:T(8,128)S(1)} %add.11.power_ref, f32[8,128]{1,0:T(8,128)S(1)} %collective-permute-done.7.added_ref), custom_call_target="tpu_custom_call" | custom-call | tf_op jit(solution)/shard_map/pallas_call | solution.py:245
  (3 shorter events, 0.0 us)
Async XLA Ops:
  0.6 4.8 %copy-start = (f32[1,1,64,128]{3,2,1,0:T(8,128)S(1)}, f32[1,1,64,128]{3,2,1,0:T(8,128)}, u32[]{:S(2)}) copy-start(f32[1,1,64,128]{3,2,1,0:T(8,128)} %param.9) | copy-start | bytes 98308
  2.3 7.2 %collective-permute-start = (f32[256,128]{1,0:T(8,128)S(1)}, f32[256,128]{1,0:T(8,128)S(1)}, u32[]{:S(2)}, u32[]{:S(2)}) collective-permute-start(f32[256,128]{1,0:T(8,128)S(1)} %get-tuple-element.24.c1_ref), channel_id=1, source_target_pairs={{0,4},{4,0},{8,12},{12,8},{16,20},{20,16},{24,28},{28,24},{1,5},{5... | collective-permute-start | bytes 393224 | tf_op jit(solution)/shard_map/ppermute | solution.py:22
  5.3 5.4 %collective-permute-start.1 = (f32[64,128]{1,0:T(8,128)S(1)}, f32[64,128]{1,0:T(8,128)S(1)}, u32[]{:S(2)}, u32[]{:S(2)}) collective-permute-start(f32[64,128]{1,0:T(8,128)S(1)} %get-tuple-element.26.g1_ref), channel_id=1, source_target_pairs={{0,4},{4,0},{8,12},{12,8},{16,20},{20,16},{24,28},{28,24},{1,5},{5... | collective-permute-start | bytes 98312 | tf_op jit(solution)/shard_map/ppermute | solution.py:22
  5.4 5.3 %collective-permute-start.2 = (f32[64,128]{1,0:T(8,128)S(1)}, f32[64,128]{1,0:T(8,128)S(1)}, u32[]{:S(2)}, u32[]{:S(2)}) collective-permute-start(f32[64,128]{1,0:T(8,128)S(1)} %bitcast.10), channel_id=1, source_target_pairs={{0,4},{4,0},{8,12},{12,8},{16,20},{20,16},{24,28},{28,24},{1,5},{5... | collective-permute-start | bytes 98312 | tf_op jit(solution)/shard_map/ppermute | solution.py:22
  11.1 12.0 %collective-permute-start.3 = (f32[576,128]{1,0:T(8,128)S(1)}, f32[576,128]{1,0:T(8,128)S(1)}, u32[]{:S(2)}, u32[]{:S(2)}) collective-permute-start(f32[576,128]{1,0:T(8,128)S(1)} %get-tuple-element.31.own_ref), channel_id=1, source_target_pairs={{0,1},{1,0},{2,3},{3,2},{4,5},{5,4},{6,7},{7,6},{8,9},{9,8},{10,11... | collective-permute-start | bytes 884744 | tf_op jit(solution)/shard_map/ppermute | solution.py:22
  11.3 3.7 %collective-permute-start.4 = (f32[8,128]{1,0:T(8,128)S(1)}, f32[8,128]{1,0:T(8,128)S(1)}, u32[]{:S(2)}, u32[]{:S(2)}) collective-permute-start(f32[8,128]{1,0:T(8,128)S(1)} %shard_map.98), channel_id=1, source_target_pairs={{0,2},{2,0},{1,3},{3,1},{4,6},{6,4},{5,7},{7,5},{8,10},{10,8},{9,1... | collective-permute-start | bytes 12296 | tf_op jit(solution)/shard_map/ppermute | solution.py:22
  14.9 3.6 %collective-permute-start.5 = (f32[8,128]{1,0:T(8,128)S(1)}, f32[8,128]{1,0:T(8,128)S(1)}, u32[]{:S(2)}, u32[]{:S(2)}) collective-permute-start(f32[8,128]{1,0:T(8,128)S(1)} %add.9), channel_id=1, source_target_pairs={{0,8},{8,0},{4,12},{12,4},{16,24},{24,16},{20,28},{28,20},{1,9},{9... | collective-permute-start | bytes 12296 | tf_op jit(solution)/shard_map/ppermute | solution.py:22
  18.5 4.5 %collective-permute-start.6 = (f32[8,128]{1,0:T(8,128)S(1)}, f32[8,128]{1,0:T(8,128)S(1)}, u32[]{:S(2)}, u32[]{:S(2)}) collective-permute-start(f32[8,128]{1,0:T(8,128)S(1)} %add.10), channel_id=1, source_target_pairs={{0,16},{16,0},{4,20},{20,4},{8,24},{24,8},{12,28},{28,12},{1,17},{... | collective-permute-start | bytes 12296 | tf_op jit(solution)/shard_map/ppermute | solution.py:22
  23.1 2.9 %collective-permute-start.7 = (f32[8,128]{1,0:T(8,128)S(1)}, f32[8,128]{1,0:T(8,128)S(1)}, u32[]{:S(2)}, u32[]{:S(2)}) collective-permute-start(f32[8,128]{1,0:T(8,128)S(1)} %add.11.power_ref), channel_id=1, source_target_pairs={{0,1},{1,0},{2,3},{3,2},{4,5},{5,4},{6,7},{7,6},{8,9},{9,8},{10,11... | collective-permute-start | bytes 12296 | tf_op jit(solution)/shard_map/ppermute | solution.py:22
